TPU v7x, 32 devices: a whole 2x2x4 slice. The times are simulated.
32 devices in a mesh: past: 4 (over y, x), second: 8 (over z, core).
Axes of the slice: x: 2, y: 2, z: 4, core: 2. Of those that a mesh axis runs over, the one named last changes fastest.
Arguments:
- resident: bfloat16 [12288, 12288], P('past', 'second'), may hold values from -6 to 6
- memory: bfloat16 [2, 384, 12288], P(None, None, 'past'), may hold values from -0.0546875 to 0.0546875
- previous: bfloat16 [2, 384, 12288], P(None, None, 'second'), may hold values from -6 to 6
- inverse_part: float32 [2, 384, 384], replicated, may hold values from -0.3125 to 0.3125
- pair_coupling: float32 [32, 32], replicated, may hold values from 0.0004510549 to 0.004510549
Outputs:
- fronts: bfloat16 [2, 384, 12288], P(None, None, 'second')
All inputs are finite; a program needn't handle non-finite values.
Results may differ from a plain program's by a relative error of at most 0.017.
Values may be sent and summed in bfloat16 or wider, within the bound.
A program may use at most 128 MiB of HBM per device.

v0:
```python
import jax
import jax.numpy as jnp
from jax import lax
from jax.sharding import PartitionSpec as P

step_size = 0.5


def orbital_flip(block, orbitals):
    row_count, col_count = block.shape
    blocks = block.reshape(row_count // orbitals, orbitals, col_count // orbitals, orbitals)
    return blocks.transpose(0, 3, 2, 1).reshape(row_count, col_count)


def solve_front(summed, prior, inverse_block):
    source = prior.astype(jnp.float32) - step_size * summed
    solved = source + jnp.dot(
        inverse_block, source, precision=lax.Precision.HIGHEST, preferred_element_type=jnp.float32
    )
    return solved.astype(jnp.bfloat16)


def self_energy(front, pair_coupling):
    orbitals = pair_coupling.shape[0]
    row_count, col_count = front.shape
    values = front.astype(jnp.float32)
    mirror = orbital_flip(values, orbitals)
    blocks = (values * values * mirror).reshape(
        row_count // orbitals, orbitals, col_count // orbitals, orbitals
    )
    return (
        (blocks * pair_coupling[None, :, None, :])
        .reshape(row_count, col_count)
        .astype(jnp.bfloat16)
    )


def per_device(resident, memory, previous, inverse_part, pair_coupling):
    past_count = lax.axis_size("past")

    def advance(memory_row, front_index):
        partial_value = jnp.dot(memory_row, resident, preferred_element_type=jnp.float32)
        summed = lax.psum(partial_value.astype(jnp.bfloat16), "past").astype(jnp.float32)
        prior_cols = previous[front_index]
        return solve_front(summed, prior_cols, inverse_part[front_index])

    front_one = advance(memory[0], 0)
    energy_one = self_energy(front_one, pair_coupling)
    band = energy_one.shape[0] // past_count
    own_rows = lax.dynamic_slice_in_dim(energy_one, lax.axis_index("past") * band, band, 0)
    wide_band = lax.all_gather(own_rows, "second", axis=1, tiled=True)
    gathered = lax.all_to_all(wide_band, "past", split_axis=1, concat_axis=0, tiled=True)
    orbitals = pair_coupling.shape[0]
    memory_next = (
        memory[1].astype(jnp.float32) + orbital_flip(gathered, orbitals).astype(jnp.float32)
    ).astype(jnp.bfloat16)
    front_two = advance(memory_next, 1)
    return jnp.stack([front_one, front_two])


def solution(mesh):
    in_specs = (P("past", "second"), P(None, None, "past"), P(None, None, "second"), P(), P())
    out_specs = P(None, None, "second")
    return jax.shard_map(
        per_device, mesh=mesh, in_specs=in_specs, out_specs=out_specs, check_vma=False
    )
```

profile of v0, /device:TPU:0, one launch (start us, length us, event | category | flops | bytes accessed | tf_op | source)
XLA Modules:
  0.0 301.7 jit_solution(1481439341360291000)
XLA Ops:
  6.5 0.0 copy-start
  6.5 0.0 all-reduce.3.cloned.1.call-start
  6.5 9.2 %convolution_convert_fusion.1 = bf16[384,1536]{1,0:T(8,128)(2,1)} fusion(bf16[3072,1536]{1,0:T(8,128)(2,1)} %param.5, bf16[2,384,3072]{2,1,0:T(8,128)(2,1)} %param.6), kind=kOutput, calls=%fused_computation.10 | convolution fusion | flops 3624468480 | bytes 12976128 | tf_op jit(solution)/shard_map/dot_general | solution.py:42
  15.8 0.0 all-reduce.3.cloned.1.call-update
  15.8 0.0 all-gather.2.cloned.1.call-start
  15.8 0.0 copy-done
  15.9 4.4 %mul.29 = f32[12,32,48,32]{3,2,1,0:T(8,128)} broadcast(f32[32,32]{1,0:T(8,128)S(1)} %copy-done), dimensions={1,3} | broadcast | bytes 2363392 | tf_op jit(solution)/shard_map/mul | solution.py:32
  20.3 6.9 %mul.30 = f32[384,1536]{1,0:T(8,128)S(1)} reshape(f32[12,32,48,32]{3,2,1,0:T(8,128)} %mul.29) | data formatting | bytes 4718592 | tf_op jit(solution)/shard_map/mul | solution.py:32
  27.2 45.8 %all-reduce.3.cloned.1.call-done = bf16[384,1536]{1,0:T(8,128)(2,1)} async-done(((bf16[384,1536]{1,0:T(8,128)(2,1)}), bf16[384,1536]{1,0:T(8,128)(2,1)}) %all-reduce.3.cloned.1.call-update) | async-done | bytes 1179664 | tf_op jit(solution)/shard_map/psum | solution.py:43
  73.0 8.3 %fusion.28 = (f32[384,1536]{1,0:T(8,128)}, bf16[384,1536]{1,0:T(8,128)(2,1)S(1)}) fusion(f32[2,384,384]{2,1,0:T(8,128)} %param.8, bf16[384,1536]{1,0:T(8,128)(2,1)} %all-reduce.3.cloned.1.call-done, bf16[2,384,1536]{2,1,0:T(8,128)(2,1)} %param.7), kind=kOutput, calls=%fused_computation.40 | convolution fusion | flops 2724397056 | bytes 8847360 | tf_op jit(solution)/shard_map/dot_general | solution.py:17
  81.3 5.0 %reshape.26 = f32[12,32,48,32]{3,2,1,0:T(8,128)} reshape(bf16[384,1536]{1,0:T(8,128)(2,1)S(1)} %get-tuple-element.6) | data formatting | bytes 3538944 | tf_op jit(solution)/shard_map/reshape | solution.py:11
  86.3 10.8 %copy.8 = f32[12,32,48,32]{3,2,1,0:T(8,128)} copy(f32[12,32,48,32]{1,2,3,0:T(8,128)} %bitcast.65) | data formatting | bytes 4718592 | tf_op jit(solution)/shard_map/transpose | solution.py:12
  97.1 7.7 %reshape.27 = f32[384,1536]{1,0:T(8,128)} reshape(f32[12,32,48,32]{3,2,1,0:T(8,128)} %copy.8) | data formatting | bytes 4718592 | tf_op jit(solution)/shard_map/reshape | solution.py:12
  104.8 2.0 fusion.21
  106.9 0.0 all-gather.2.cloned.1.call-update
  106.9 0.0 all-reduce.5.cloned.1.call-start
  106.9 31.5 %all-gather.2.cloned.1.call-done = bf16[96,12288]{1,0:T(8,128)(2,1)} async-done(((bf16[96,1536]{1,0:T(8,128)(2,1)}), bf16[96,12288]{1,0:T(8,128)(2,1)}) %all-gather.2.cloned.1.call-update) | async-done | bytes 2359312 | tf_op jit(solution)/shard_map/all_gather | solution.py:51
  138.5 1.8 copy.15
  140.3 32.0 %all_to_all.13 = bf16[96,4,3072]{2,0,1:T(8,128)(2,1)S(1)} all-to-all(bf16[96,4,3072]{2,0,1:T(8,128)(2,1)S(1)} %bitcast.66), channel_id=1, replica_groups=mesh['past'=4,'second'=8] {'past'}, dimensions={1} | all-to-all | bytes 4718592 | tf_op jit(solution)/shard_map/all_to_all | solution.py:52
  172.4 2.7 convert_bitcast_fusion
  175.1 12.3 %reshape.32 = f32[12,32,96,32]{3,2,1,0:T(8,128)} reshape(f32[4,96,3072]{2,1,0:T(8,128)} %convert_bitcast_fusion) | data formatting | bytes 9437184 | tf_op jit(solution)/shard_map/convert_element_type | solution.py:55
  187.4 22.5 %copy.10 = f32[12,32,96,32]{3,2,1,0:T(8,128)} copy(f32[12,32,96,32]{1,2,3,0:T(8,128)} %bitcast.64) | data formatting | bytes 9437184 | tf_op jit(solution)/shard_map/convert_element_type | solution.py:55
  209.9 14.6 %reshape.31 = f32[384,3072]{1,0:T(8,128)} reshape(f32[12,32,96,32]{3,2,1,0:T(8,128)} %copy.10) | data formatting | bytes 9437184 | tf_op jit(solution)/shard_map/convert_element_type | solution.py:55
  224.4 0.0 copy-start.1
  224.5 10.7 %convolution_convert_fusion = bf16[384,1536]{1,0:T(8,128)(2,1)} fusion(bf16[3072,1536]{1,0:T(8,128)(2,1)} %param.5, f32[384,3072]{1,0:T(8,128)} %reshape.31, bf16[2,384,3072]{2,1,0:T(8,128)(2,1)} %param.6), kind=kOutput, calls=%fused_computation.9 | convolution fusion | flops 3628007424 | bytes 17694720 | tf_op jit(solution)/shard_map/dot_general | solution.py:42
  235.2 0.0 all-reduce.5.cloned.1.call-update
  235.2 52.3 %all-reduce.5.cloned.1.call-done = bf16[384,1536]{1,0:T(8,128)(2,1)} async-done(((bf16[384,1536]{1,0:T(8,128)(2,1)}), bf16[384,1536]{1,0:T(8,128)(2,1)}) %all-reduce.5.cloned.1.call-update) | async-done | bytes 1179664 | tf_op jit(solution)/shard_map/psum | solution.py:43
  287.5 0.0 copy-done.1
  287.5 6.1 %fusion.5 = bf16[1,384,1536]{2,1,0:T(8,128)(2,1)S(1)} fusion(bf16[384,1536]{1,0:T(8,128)(2,1)} %all-reduce.5.cloned.1.call-done, bf16[2,384,1536]{2,1,0:T(8,128)(2,1)S(1)} %copy-done.1, f32[2,384,384]{2,1,0:T(8,128)} %param.8), kind=kOutput, calls=%fused_computation.11 | convolution fusion | flops 2723807232 | bytes 6488064 | tf_op jit(solution)/shard_map/dot_general | solution.py:17
  293.6 1.6 pad_maximum_fusion
Async XLA Ops:
  6.5 9.3 %copy-start = (f32[32,32]{1,0:T(8,128)S(1)}, f32[32,32]{1,0:T(8,128)}, u32[]{:S(2)}) copy-start(f32[32,32]{1,0:T(8,128)} %param.9) | copy-start | bytes 12292
  6.5 66.5 %all-reduce.3.cloned.1.call-start = ((), (), s32[]{:S(2)}) async-start(), calls=%async_computation.1 | async-start | bytes 2359296 | tf_op jit(solution)/shard_map/psum | solution.py:43
  15.8 122.7 %all-gather.2.cloned.1.call-start = ((), (), s32[]{:S(2)}) async-start(), calls=%async_computation.2 | async-start | bytes 2654208 | tf_op jit(solution)/shard_map/all_gather | solution.py:51
  106.9 180.6 %all-reduce.5.cloned.1.call-start = ((), (), s32[]{:S(2)}) async-start(), calls=%async_computation.3 | async-start | bytes 2359296 | tf_op jit(solution)/shard_map/psum | solution.py:43
  224.4 63.0 %copy-start.1 = (bf16[2,384,1536]{2,1,0:T(8,128)(2,1)S(1)}, bf16[2,384,1536]{2,1,0:T(8,128)(2,1)}, u32[]{:S(2)}) copy-start(bf16[2,384,1536]{2,1,0:T(8,128)(2,1)} %param.7) | copy-start | bytes 7077892
Sparse Core Ops, SparseCore 0:
  15.9 57.0 all-reduce.2
  107.0 31.4 all-gather.1
  235.3 52.1 all-reduce.4
where the time goes:
time: 303 us; the launch traced here: 302 us
  waiting for transfers between devices  130 us (43%)
  local copies, waits for them, and re-layouts  86.1 us (28%)
  matrix products  34.3 us (11%)
  blocking collectives  32 us (11%)
  between operations  13.2 us (4%)
  other arithmetic  6.39 us (2%)
    psum x2, waiting for transfers between devices, advance(): lax.psum(partial_value.astype(jnp.bfloat16), 'past').astype(jnp.float32)  98.1 us
    convert_element_type x3, local copies, waits for them, and re-layouts, per_device(): orbital_flip(gathered, orbitals).astype(jnp.float32)  49.4 us
    all_to_all x1, blocking collectives, per_device(): lax.all_to_all(wide_band, 'past', split_axis=1, concat_axis=0, tiled=True)  32 us
    all_gather x1, waiting for transfers between devices, per_device(): wide_band = lax.all_gather(own_rows, 'second', axis=1, tiled=True)  31.5 us
    dot_general x2, matrix products, advance(): jnp.dot(memory_row, resident, preferred_element_type=jnp.float32)  19.9 us
    dot_general x2, matrix products, solve_front(): jnp.dot(inverse_block, source, precision=lax.Precision.HIGHEST, preferred...  14.3 us
    mul x2, local copies, waits for them, and re-layouts, self_energy(): blocks * pair_coupling[None, :, None, :]  11.3 us
    transpose x1, local copies, waits for them, and re-layouts, orbital_flip(): return blocks.transpose(0, 3, 2, 1).reshape(row_count, col_count)  10.8 us
  transfers between devices with their start and end apart: 3, of which 3 were waited for; matrix products, arithmetic and copies ran while one was open for 4% of the time, Pallas kernels for 0%

commit v1 on v0

--- a/solution.py
+++ b/solution.py
@@ -40,7 +40,9 @@
 
     def advance(memory_row, front_index):
         partial_value = jnp.dot(memory_row, resident, preferred_element_type=jnp.float32)
-        summed = lax.psum(partial_value.astype(jnp.bfloat16), "past").astype(jnp.float32)
+        summed = jnp.sum(lax.all_gather(partial_value.astype(jnp.bfloat16), "past"), axis=0).astype(
+            jnp.float32
+        )
         prior_cols = previous[front_index]
         return solve_front(summed, prior_cols, inverse_part[front_index])
 

time: 303 us -> 316 us (1.043)
  other arithmetic: 6.39 us -> 14.7 us
  waiting for transfers between devices: 130 us -> 135 us
    all_gather x0 -> x2, waiting for transfers between devices: none -> 103 us  [advance(): lax.all_gather(partial_value.astype(jnp.bfloat16), 'past')]
    psum x2 -> x0, waiting for transfers between devices: 98.1 us -> none  [advance(): lax.psum(partial_value.astype(jnp.bfloat16), 'past').astype(jnp.float32)]
    reduce_sum x0 -> x2, other arithmetic: none -> 8.26 us  [advance(): jnp.sum(lax.all_gather(partial_value.astype(jnp.bfloat16), 'past'), axis=0)]
where the time goes in v1:
time: 316 us; the launch traced here: 315 us
  waiting for transfers between devices  135 us (43%)
  local copies, waits for them, and re-layouts  86.1 us (27%)
  matrix products  34 us (11%)
  blocking collectives  32 us (10%)
  other arithmetic  14.7 us (5%)
  between operations  13.2 us (4%)
    all_gather x2, waiting for transfers between devices, advance(): lax.all_gather(partial_value.astype(jnp.bfloat16), 'past')  103 us
    convert_element_type x3, local copies, waits for them, and re-layouts, per_device(): orbital_flip(gathered, orbitals).astype(jnp.float32)  49.4 us
    all_to_all x1, blocking collectives, per_device(): lax.all_to_all(wide_band, 'past', split_axis=1, concat_axis=0, tiled=True)  32 us
    all_gather x1, waiting for transfers between devices, per_device(): wide_band = lax.all_gather(own_rows, 'second', axis=1, tiled=True)  31.5 us
    dot_general x2, matrix products, advance(): jnp.dot(memory_row, resident, preferred_element_type=jnp.float32)  19.8 us
    dot_general x2, matrix products, solve_front(): jnp.dot(inverse_block, source, precision=lax.Precision.HIGHEST, preferred...  14.2 us
    mul x2, local copies, waits for them, and re-layouts, self_energy(): blocks * pair_coupling[None, :, None, :]  11.4 us
    transpose x1, local copies, waits for them, and re-layouts, orbital_flip(): return blocks.transpose(0, 3, 2, 1).reshape(row_count, col_count)  10.8 us
  transfers between devices with their start and end apart: 3, of which 3 were waited for; matrix products, arithmetic and copies ran while one was open for 4% of the time, Pallas kernels for 0%

profile of v1, /device:TPU:0, one launch (start us, length us, event | category | flops | bytes accessed | tf_op | source)
XLA Modules:
  0.0 314.9 jit_solution(1704897174596839564)
XLA Ops:
  6.5 0.0 copy-start
  6.5 0.0 all-gather.8.cloned.1.call-start
  6.5 9.2 %convolution_convert_fusion.1 = bf16[384,1536]{1,0:T(8,128)(2,1)} fusion(bf16[3072,1536]{1,0:T(8,128)(2,1)} %param.5, bf16[2,384,3072]{2,1,0:T(8,128)(2,1)} %param.6), kind=kOutput, calls=%fused_computation.14 | convolution fusion | flops 3624468480 | bytes 12976128 | tf_op jit(solution)/shard_map/dot_general | solution.py:42
  15.8 0.0 all-gather.8.cloned.1.call-update
  15.8 0.0 all-gather.6.cloned.1.call-start
  15.8 0.0 copy-done
  15.9 4.4 %mul.50 = f32[12,32,48,32]{3,2,1,0:T(8,128)} broadcast(f32[32,32]{1,0:T(8,128)S(1)} %copy-done), dimensions={1,3} | broadcast | bytes 2363392 | tf_op jit(solution)/shard_map/mul | solution.py:32
  20.3 6.9 %mul.51 = f32[384,1536]{1,0:T(8,128)S(1)} reshape(f32[12,32,48,32]{3,2,1,0:T(8,128)} %mul.50) | data formatting | bytes 4718592 | tf_op jit(solution)/shard_map/mul | solution.py:32
  27.2 48.4 %all-gather.8.cloned.1.call-done = bf16[1536,1536]{1,0:T(8,128)(2,1)} async-done(((bf16[384,1536]{1,0:T(8,128)(2,1)}), bf16[1536,1536]{1,0:T(8,128)(2,1)}) %all-gather.8.cloned.1.call-update) | async-done | bytes 4718608 | tf_op jit(solution)/shard_map/all_gather | solution.py:43
  75.6 4.4 %reduce_sum.24 = bf16[384,1536]{1,0:T(8,128)(2,1)} reduce(bf16[4,384,1536]{2,1,0:T(8,128)(2,1)} %bitcast.87, bf16[]{:T(256)} %constant.6.clone.1), dimensions={0}, to_apply=%region_0.0 | reduce | flops 1769472 | bytes 5898242 | tf_op jit(solution)/shard_map/reduce_sum | solution.py:43
  80.0 8.2 %fusion.34 = (f32[384,1536]{1,0:T(8,128)}, bf16[384,1536]{1,0:T(8,128)(2,1)S(1)}) fusion(f32[2,384,384]{2,1,0:T(8,128)} %param.8, bf16[384,1536]{1,0:T(8,128)(2,1)} %reduce_sum.24, bf16[2,384,1536]{2,1,0:T(8,128)(2,1)} %param.7), kind=kOutput, calls=%fused_computation.46 | convolution fusion | flops 2724397056 | bytes 8847360 | tf_op jit(solution)/shard_map/dot_general | solution.py:17
  88.3 5.0 %reshape.54 = f32[12,32,48,32]{3,2,1,0:T(8,128)} reshape(bf16[384,1536]{1,0:T(8,128)(2,1)S(1)} %get-tuple-element.6) | data formatting | bytes 3538944 | tf_op jit(solution)/shard_map/reshape | solution.py:11
  93.2 10.8 %copy.8 = f32[12,32,48,32]{3,2,1,0:T(8,128)} copy(f32[12,32,48,32]{1,2,3,0:T(8,128)} %bitcast.85) | data formatting | bytes 4718592 | tf_op jit(solution)/shard_map/transpose | solution.py:12
  104.1 7.7 %reshape.55 = f32[384,1536]{1,0:T(8,128)} reshape(f32[12,32,48,32]{3,2,1,0:T(8,128)} %copy.8) | data formatting | bytes 4718592 | tf_op jit(solution)/shard_map/reshape | solution.py:12
  111.8 2.0 fusion.27
  113.8 0.0 all-gather.6.cloned.1.call-update
  113.9 0.0 all-gather.10.cloned.1.call-start
  113.9 31.5 %all-gather.6.cloned.1.call-done = bf16[96,12288]{1,0:T(8,128)(2,1)} async-done(((bf16[96,1536]{1,0:T(8,128)(2,1)}), bf16[96,12288]{1,0:T(8,128)(2,1)}) %all-gather.6.cloned.1.call-update) | async-done | bytes 2359312 | tf_op jit(solution)/shard_map/all_gather | solution.py:53
  145.5 1.8 copy.15
  147.3 32.0 %all_to_all.13 = bf16[96,4,3072]{2,0,1:T(8,128)(2,1)S(1)} all-to-all(bf16[96,4,3072]{2,0,1:T(8,128)(2,1)S(1)} %bitcast.86), channel_id=1, replica_groups=mesh['past'=4,'second'=8] {'past'}, dimensions={1} | all-to-all | bytes 4718592 | tf_op jit(solution)/shard_map/all_to_all | solution.py:54
  179.3 2.7 convert_bitcast_fusion
  182.1 12.3 %reshape.60 = f32[12,32,96,32]{3,2,1,0:T(8,128)} reshape(f32[4,96,3072]{2,1,0:T(8,128)} %convert_bitcast_fusion) | data formatting | bytes 9437184 | tf_op jit(solution)/shard_map/convert_element_type | solution.py:57
  194.4 22.5 %copy.10 = f32[12,32,96,32]{3,2,1,0:T(8,128)} copy(f32[12,32,96,32]{1,2,3,0:T(8,128)} %bitcast.84) | data formatting | bytes 9437184 | tf_op jit(solution)/shard_map/convert_element_type | solution.py:57
  216.9 14.6 %reshape.59 = f32[384,3072]{1,0:T(8,128)} reshape(f32[12,32,96,32]{3,2,1,0:T(8,128)} %copy.10) | data formatting | bytes 9437184 | tf_op jit(solution)/shard_map/convert_element_type | solution.py:57
  231.4 10.6 %convolution_convert_fusion = bf16[384,1536]{1,0:T(8,128)(2,1)} fusion(bf16[3072,1536]{1,0:T(8,128)(2,1)} %param.5, f32[384,3072]{1,0:T(8,128)} %reshape.59, bf16[2,384,3072]{2,1,0:T(8,128)(2,1)} %param.6), kind=kOutput, calls=%fused_computation.13 | convolution fusion | flops 3628007424 | bytes 17694720 | tf_op jit(solution)/shard_map/dot_general | solution.py:42
  242.0 0.0 all-gather.10.cloned.1.call-update
  242.0 54.9 %all-gather.10.cloned.1.call-done = bf16[1536,1536]{1,0:T(8,128)(2,1)} async-done(((bf16[384,1536]{1,0:T(8,128)(2,1)}), bf16[1536,1536]{1,0:T(8,128)(2,1)}) %all-gather.10.cloned.1.call-update) | async-done | bytes 4718608 | tf_op jit(solution)/shard_map/all_gather | solution.py:43
  296.9 0.0 copy-start.1
  296.9 3.8 %reduce_sum.25 = bf16[384,1536]{1,0:T(8,128)(2,1)S(1)} reduce(bf16[4,384,1536]{2,1,0:T(8,128)(2,1)} %bitcast.88, bf16[]{:T(256)} %constant.6.clone.1), dimensions={0}, to_apply=%region_1.0 | reduce | flops 1769472 | bytes 5898242 | tf_op jit(solution)/shard_map/reduce_sum | solution.py:43
  300.7 0.0 copy-done.1
  300.8 6.0 %fusion.5 = bf16[1,384,1536]{2,1,0:T(8,128)(2,1)S(1)} fusion(bf16[384,1536]{1,0:T(8,128)(2,1)S(1)} %reduce_sum.25, bf16[2,384,1536]{2,1,0:T(8,128)(2,1)} %param.7, f32[2,384,384]{2,1,0:T(8,128)S(1)} %copy-done.1), kind=kOutput, calls=%fused_computation.15 | convolution fusion | flops 2723807232 | bytes 6488064 | tf_op jit(solution)/shard_map/dot_general | solution.py:17
  306.8 1.6 pad_maximum_fusion
Async XLA Ops:
  6.5 9.3 %copy-start = (f32[32,32]{1,0:T(8,128)S(1)}, f32[32,32]{1,0:T(8,128)}, u32[]{:S(2)}) copy-start(f32[32,32]{1,0:T(8,128)} %param.9) | copy-start | bytes 12292
  6.5 69.1 %all-gather.8.cloned.1.call-start = ((), (), s32[]{:S(2)}) async-start(), calls=%async_computation.2 | async-start | bytes 5898240 | tf_op jit(solution)/shard_map/all_gather | solution.py:43
  15.8 129.7 %all-gather.6.cloned.1.call-start = ((), (), s32[]{:S(2)}) async-start(), calls=%async_computation.1 | async-start | bytes 2654208 | tf_op jit(solution)/shard_map/all_gather | solution.py:53
  113.9 183.0 %all-gather.10.cloned.1.call-start = ((), (), s32[]{:S(2)}) async-start(), calls=%async_computation.3 | async-start | bytes 5898240 | tf_op jit(solution)/shard_map/all_gather | solution.py:43
  296.9 3.8 %copy-start.1 = (f32[2,384,384]{2,1,0:T(8,128)S(1)}, f32[2,384,384]{2,1,0:T(8,128)}, u32[]{:S(2)}) copy-start(f32[2,384,384]{2,1,0:T(8,128)} %param.8) | copy-start | bytes 3538948
Sparse Core Ops, SparseCore 0:
  15.9 59.6 all-gather.7
  114.0 31.4 all-gather.5
  242.1 54.7 all-gather.9
